TPU v7x, 32 devices: a whole 2x2x4 slice. The times are simulated.
32 devices in a mesh: seq: 16 (over z, x, core), ch: 2 (over y).
Axes of the slice: x: 2, y: 2, z: 4, core: 2. Of those that a mesh axis runs over, the one named last changes fastest.
Arguments:
- tokens: bfloat16 [131072, 1024], P('seq', 'ch'), may hold values from -6 to 6
- right_block: bfloat16 [1024, 1024], P('seq'), may hold values from -0.1875 to 0.1875
- twiddle: bfloat16 [128, 1024], P('seq'), may hold values from -4 to 4
- left_block: bfloat16 [128, 128], replicated, may hold values from -0.5 to 0.5
- gain: float32 [1024], replicated, may hold values from 0.1 to 1.9
- mix_weight: bfloat16 [4, 256, 256], replicated, may hold values from -0.375 to 0.375
Outputs:
- layer_out: bfloat16 [131072, 1024], P(('seq', 'ch'))
All inputs are finite; a program needn't handle non-finite values.
Results may differ from a plain program's by a relative error of at most 0.007.
Values may be sent and summed in bfloat16 or wider, within the bound.
No kernel may reach another device: no remote copies, remote signals or barrier semaphores. Data moves between devices by JAX's collectives and lax.ppermute only.
A program may use at most 128 MiB of HBM per device.

v0:
```python
import jax
import jax.numpy as jnp
from jax import lax
from jax.sharding import PartitionSpec as P


def body(tokens, right_block, twiddle, left_block, gain, mix_weight):
    row_width = right_block.shape[1]
    row_count = tokens.shape[0] // row_width
    local_width = tokens.shape[1]
    inputs = tokens.reshape(row_count, row_width, local_width)
    whole_right = lax.all_gather(right_block, "seq", axis=0, tiled=True)
    first_section = jnp.einsum(
        "abc,bk->akc", inputs, whole_right, preferred_element_type=jnp.float32
    )
    spread = (first_section * twiddle.astype(jnp.float32)[:, :, None]).astype(jnp.bfloat16)
    mixed_rows = jnp.einsum(
        "ij,jbc->ibc",
        left_block,
        lax.all_to_all(spread, "seq", split_axis=1, concat_axis=0, tiled=True),
        preferred_element_type=jnp.float32,
    ).astype(jnp.bfloat16)
    sequence_mixed = lax.all_to_all(mixed_rows, "seq", split_axis=0, concat_axis=1, tiled=True)
    gated = (sequence_mixed.astype(jnp.float32) * jax.nn.silu(inputs.astype(jnp.float32))).astype(
        jnp.bfloat16
    )
    ch_count = lax.axis_size("ch")
    pieces = gated.reshape(ch_count, row_count * row_width // ch_count, local_width)
    shard_piece = lax.all_to_all(pieces, "ch", split_axis=0, concat_axis=2, tiled=True)
    values = shard_piece.astype(jnp.float32)
    inverse_rms = lax.rsqrt(jnp.mean(values * values, axis=-1, keepdims=True) + 1e-05)
    normed = (values * inverse_rms * gain).astype(jnp.bfloat16)
    block_count = mix_weight.shape[0]
    block_width = mix_weight.shape[1]
    normed = normed.reshape(shard_piece.shape[0], shard_piece.shape[1], block_count, block_width)
    result = jnp.einsum("otki,kij->otkj", normed, mix_weight, preferred_element_type=jnp.float32)
    mixed_out = result.astype(jnp.bfloat16).reshape(shard_piece.shape)
    return mixed_out.reshape(mixed_out.shape[1], mixed_out.shape[2])


def solution(mesh):
    in_specs = (P("seq", "ch"), P("seq", None), P("seq", None), P(), P(), P())
    out_specs = P(("seq", "ch"), None)
    return jax.shard_map(body, mesh=mesh, in_specs=in_specs, out_specs=out_specs, check_vma=False)
```

profile of v0, /device:TPU:0, one launch (start us, length us, event | category | flops | bytes accessed | tf_op | source)
XLA Modules:
  0.0 688.4 jit_solution(9891246923339993870)
XLA Ops:
  6.5 0.0 copy-start
  6.5 0.0 all-gather.2.cloned.1.call-start
  6.5 0.7 all-gather.2.cloned.1.call-update
  7.3 0.7 convert_element_type.77
  8.0 45.7 %all-gather.2.cloned.1.call-done = bf16[1024,1024]{1,0:T(8,128)(2,1)} async-done(((bf16[64,1024]{1,0:T(8,128)(2,1)}), bf16[1024,1024]{1,0:T(8,128)(2,1)}) %all-gather.2.cloned.1.call-update) | async-done | bytes 2097168 | tf_op jit(solution)/shard_map/all_gather | solution.py:12
  53.7 14.9 %fusion.5 = bf16[8,1024,512]{2,1,0:T(8,128)(2,1)} fusion(bf16[8,1024,512]{2,1,0:T(8,128)(2,1)} %bitcast.44, f32[8,1024]{1,0:T(8,128)S(1)} %convert_element_type.77, bf16[1024,1024]{1,0:T(8,128)(2,1)} %all-gather.2.cloned.1.call-done), kind=kOutput, calls=%fused_computation.11 | convolution fusion | flops 8598323200 | bytes 18907136 | tf_op jit(solution)/shard_map/abc,bk->akc/dot_general | solution.py:13
  68.6 11.3 %copy.26 = bf16[8,1024,512]{2,0,1:T(8,128)(2,1)} copy(bf16[8,1024,512]{2,1,0:T(8,128)(2,1)} %fusion.5) | data formatting | bytes 16777216 | tf_op jit(solution)/shard_map/convert_element_type | solution.py:16
  79.9 186.7 %all_to_all.36 = bf16[8,1024,512]{2,0,1:T(8,128)(2,1)} all-to-all(bf16[8,1024,512]{2,0,1:T(8,128)(2,1)} %copy.26), channel_id=1, replica_groups=mesh['seq'=16,'ch'=2] {'seq'}, dimensions={1} | all-to-all | bytes 16777216 | tf_op jit(solution)/shard_map/all_to_all | solution.py:20
  266.6 0.0 copy-start.1
  266.6 10.3 %copy.28 = bf16[16,8,64,512]{3,2,1,0:T(8,128)(2,1)} copy(bf16[16,8,64,512]{3,1,2,0:T(8,128)(2,1)} %bitcast.42) | data formatting | bytes 16777216 | tf_op jit(solution)/shard_map/all_to_all | solution.py:20
  276.9 0.0 copy-done.1
  276.9 22.3 %convert_bitcast_fusion.2 = bf16[128,64,512]{0,2,1:T(8,128)(2,1)} fusion(bf16[128,64,512]{2,1,0:T(8,128)(2,1)} %bitcast.43, bf16[128,128]{1,0:T(8,128)(2,1)S(1)} %copy-done.1), kind=kOutput, calls=%fused_computation.19 | convolution fusion | flops 1077936128 | bytes 16809984 | tf_op jit(solution)/shard_map/ij,jbc->ibc/dot_general | solution.py:17
  299.2 12.6 %copy.30 = bf16[128,64,512]{2,1,0:T(8,128)(2,1)} copy(bf16[128,64,512]{0,2,1:T(8,128)(2,1)} %convert_bitcast_fusion.2) | data formatting | bytes 16777216 | tf_op jit(solution)/shard_map/convert_element_type | solution.py:22
  311.9 187.2 %all_to_all.37 = bf16[128,64,512]{2,1,0:T(8,128)(2,1)} all-to-all(bf16[128,64,512]{2,1,0:T(8,128)(2,1)} %copy.30), channel_id=1, replica_groups=mesh['seq'=16,'ch'=2] {'seq'}, dimensions={0} | all-to-all | bytes 16777216 | tf_op jit(solution)/shard_map/all_to_all | solution.py:23
  499.1 0.0 slice-start
  499.1 11.7 %convert_bitcast_fusion.1 = f32[8,16,64,512]{3,2,0,1:T(8,128)} fusion(bf16[16,8,64,512]{3,2,1,0:T(8,128)(2,1)} %bitcast.40), kind=kLoop, calls=%fused_computation.9 | loop fusion | flops 4194304 | bytes 25165824 | tf_op jit(solution)/shard_map/convert_element_type | solution.py:24
  510.8 0.0 slice-start.1
  510.8 7.1 %copy.31 = f32[8,16,64,512]{3,2,1,0:T(8,128)S(1)} copy(f32[8,16,64,512]{3,2,0,1:T(8,128)} %convert_bitcast_fusion.1) | data formatting | bytes 33554432 | tf_op jit(solution)/shard_map/convert_element_type | solution.py:24
  517.9 0.0 slice-done
  518.0 0.0 slice-done.1
  518.0 7.0 %fusion.6 = bf16[2,4096,512]{2,1,0:T(8,128)(2,1)} fusion(f32[2,4096,512]{2,1,0:T(8,128)S(1)} %bitcast.39, bf16[2,4096,512]{2,1,0:T(8,128)(2,1)S(1)} %bitcast.47), kind=kLoop, calls=%fused_computation.13 | loop fusion | flops 29360128 | bytes 33554432 | tf_op jit(solution)/shard_map/convert_element_type | solution.py:24
  525.0 0.0 copy-start.2
  525.0 7.3 %all-to-all-start.2 = ((bf16[2,4096,512]{2,1,0:T(8,128)(2,1)}), bf16[2,4096,512]{2,1,0:T(8,128)(2,1)}, u32[]{:S(2)}, u32[]{:S(2)}) async-start(bf16[2,4096,512]{2,1,0:T(8,128)(2,1)} %fusion.6), calls=%async_computation.2 | async-start | bytes 16777216 | tf_op jit(solution)/shard_map/all_to_all | solution.py:29
  532.3 0.0 copy-done.2
  532.3 93.7 %all-to-all-done.2 = bf16[2,4096,512]{2,1,0:T(8,128)(2,1)} async-done(((bf16[2,4096,512]{2,1,0:T(8,128)(2,1)}), bf16[2,4096,512]{2,1,0:T(8,128)(2,1)}, u32[]{:S(2)}, u32[]{:S(2)}) %all-to-all-start.2) | async-done | bytes 8388640 | tf_op jit(solution)/shard_map/all_to_all | solution.py:29
  626.0 5.1 fusion
  631.1 11.5 %convert_bitcast_fusion = f32[1,4096,2,512]{3,1,2,0:T(8,128)} fusion(bf16[2,4096,512]{2,1,0:T(8,128)(2,1)} %all-to-all-done.2), kind=kLoop, calls=%fused_computation.3 | loop fusion | flops 4194304 | bytes 25165824 | tf_op jit(solution)/shard_map/convert_element_type | solution.py:30
  642.7 17.6 %copy.32 = f32[1,4096,2,512]{1,3,2,0:T(8,128)} copy(f32[1,4096,2,512]{3,1,2,0:T(8,128)} %convert_bitcast_fusion) | data formatting | bytes 33554432 | tf_op jit(solution)/shard_map/convert_element_type | solution.py:30
  660.2 0.0 copy-done
  660.2 9.2 %fusion.12 = bf16[4,4096,256]{1,2,0:T(8,128)(2,1)} fusion(bf16[4,256,256]{2,1,0:T(8,128)(2,1)S(1)} %copy-done, f32[4096,4,256]{0,2,1:T(8,128)} %bitcast.38, f32[4,256]{1,0:T(4,128)S(1)} %mul.58, f32[4096]{0:T(1024)S(1)} %add_rsqrt_fusion), kind=kOutput, calls=%fused_computation.20 | convolution fusion | flops 2164260864 | bytes 25710592 | tf_op jit(solution)/shard_map/otki,kij->otkj/dot_general | solution.py:36
  669.4 11.9 %copy.35 = bf16[4096,1024]{1,0:T(8,128)(2,1)} copy(bf16[4096,1024]{0,1:T(8,128)(2,1)} %bitcast.41) | data formatting | bytes 16777216 | tf_op jit(solution)/shard_map/reshape;reshape | solution.py:38
  (3 shorter events, 0.0 us)
Async XLA Ops:
  6.5 653.7 %copy-start = (bf16[4,256,256]{2,1,0:T(8,128)(2,1)S(1)}, bf16[4,256,256]{2,1,0:T(8,128)(2,1)}, u32[]{:S(2)}) copy-start(bf16[4,256,256]{2,1,0:T(8,128)(2,1)} %param.11) | copy-start | bytes 1572868
  6.5 47.2 %all-gather.2.cloned.1.call-start = ((), (), s32[]{:S(2)}) async-start(), calls=%async_computation.3 | async-start | bytes 2228224 | tf_op jit(solution)/shard_map/all_gather | solution.py:12
  266.6 10.3 %copy-start.1 = (bf16[128,128]{1,0:T(8,128)(2,1)S(1)}, bf16[128,128]{1,0:T(8,128)(2,1)}, u32[]{:S(2)}) copy-start(bf16[128,128]{1,0:T(8,128)(2,1)} %param.9) | copy-start | bytes 98308
  499.1 18.9 %slice-start = ((s8[8388608]{0:T(1024)(128)(4,1)}), s8[4194304]{0:T(1024)(128)(4,1)S(1)}, s32[]{:S(2)}) async-start(s8[8388608]{0:T(1024)(128)(4,1)} %bitcast.45), calls=%async_computation.4 | async-start | bytes 8388608
  510.8 7.1 %slice-start.1 = ((s8[8388608]{0:T(1024)(128)(4,1)}), s8[4194304]{0:T(1024)(128)(4,1)S(1)}, s32[]{:S(2)}) async-start(s8[8388608]{0:T(1024)(128)(4,1)} %bitcast.45), calls=%async_computation.5 | async-start | bytes 8388608
  525.0 7.3 %copy-start.2 = (f32[1024]{0:T(1024)S(1)}, f32[1024]{0:T(1024)}, u32[]{:S(2)}) copy-start(f32[1024]{0:T(1024)} %param.10) | copy-start | bytes 12292
  525.0 101.0 %all-to-all-start.2 = ((bf16[2,4096,512]{2,1,0:T(8,128)(2,1)}), bf16[2,4096,512]{2,1,0:T(8,128)(2,1)}, u32[]{:S(2)}, u32[]{:S(2)}) async-start(bf16[2,4096,512]{2,1,0:T(8,128)(2,1)} %fusion.6), calls=%async_computation.2 | async-start | bytes 16777216 | tf_op jit(solution)/shard_map/all_to_all | solution.py:29
Sparse Core Ops, SparseCore 0:
  9.5 44.1 all-gather.1
where the time goes:
time: 697 us; the launch traced here: 688 us
  blocking collectives  374 us (54%)
  waiting for transfers between devices  140 us (20%)
  local copies, waits for them, and re-layouts  70.9 us (10%)
  matrix products  46.4 us (7%)
  other arithmetic  36.1 us (5%)
  between operations  13.7 us (2%)
  starting transfers between devices  7.29 us (1%)
    all_to_all x1, blocking collectives, body(): lax.all_to_all(mixed_rows, 'seq', split_axis=0, concat_axis=1, tiled=True)  187 us
    all_to_all x1, blocking collectives, body(): lax.all_to_all(spread, 'seq', split_axis=1, concat_axis=0, tiled=True)  187 us
    all_to_all x1, waiting for transfers between devices, body(): lax.all_to_all(pieces, 'ch', split_axis=0, concat_axis=2, tiled=True)  93.7 us
    all_gather x1, waiting for transfers between devices, body(): whole_right = lax.all_gather(right_block, 'seq', axis=0, tiled=True)  45.7 us
    dot_general x1, matrix products, body(): jnp.einsum('ij,jbc->ibc', left_block, lax.all_to_all(spread, 'seq', split...  22.3 us
    convert_element_type x1, local copies, waits for them, and re-layouts, body(): values = shard_piece.astype(jnp.float32)  17.6 us
    dot_general x1, matrix products, body(): jnp.einsum('abc,bk->akc', inputs, whole_right, preferred_element_type=jnp...  14.9 us
  transfers between devices with their start and end apart: 2, of which 2 were waited for; matrix products, arithmetic and copies ran while one was open for 0% of the time, Pallas kernels for 0%

commit v1 on v0

--- a/solution.py
+++ b/solution.py
@@ -2,6 +2,13 @@
 import jax.numpy as jnp
 from jax import lax
 from jax.sharding import PartitionSpec as P
+
+
+def trade_parts(block, axis, split, join):
+    size = lax.axis_size(axis)
+    blocks = jnp.stack(jnp.split(block, size, axis=split), axis=0)
+    blocks = lax.all_to_all(blocks, axis, split_axis=0, concat_axis=0)
+    return jnp.concatenate(blocks, axis=join)
 
 
 def body(tokens, right_block, twiddle, left_block, gain, mix_weight):
@@ -17,7 +24,7 @@
     mixed_rows = jnp.einsum(
         "ij,jbc->ibc",
         left_block,
-        lax.all_to_all(spread, "seq", split_axis=1, concat_axis=0, tiled=True),
+        trade_parts(spread, "seq", 1, 0),
         preferred_element_type=jnp.float32,
     ).astype(jnp.bfloat16)
     sequence_mixed = lax.all_to_all(mixed_rows, "seq", split_axis=0, concat_axis=1, tiled=True)

time: 697 us -> 661 us (0.948); the launches traced: 688 us -> 660 us
  local copies, waits for them, and re-layouts: 70.9 us -> 49.9 us
    convert_element_type x2 -> x1, local copies, waits for them, and re-layouts: 24 us -> 12.5 us  [body(): mixed_rows = jnp.einsum('ij,jbc->ibc', left_block, trade_parts(spread, 's...]
    all_to_all x1 -> x0, local copies, waits for them, and re-layouts: 10.3 us -> none  [body(): lax.all_to_all(spread, 'seq', split_axis=1, concat_axis=0, tiled=True)]
where the time goes in v1:
time: 661 us; the launch traced here: 660 us
  blocking collectives  373 us (56%)
  waiting for transfers between devices  140 us (21%)
  local copies, waits for them, and re-layouts  49.9 us (8%)
  matrix products  39.7 us (6%)
  other arithmetic  36.1 us (5%)
  between operations  13.6 us (2%)
  starting transfers between devices  7.29 us (1%)
    all_to_all x1, blocking collectives, body(): lax.all_to_all(mixed_rows, 'seq', split_axis=0, concat_axis=1, tiled=True)  188 us
    all_to_all x1, blocking collectives, trade_parts(): blocks = lax.all_to_all(blocks, axis, split_axis=0, concat_axis=0)  185 us
    all_to_all x1, waiting for transfers between devices, body(): lax.all_to_all(pieces, 'ch', split_axis=0, concat_axis=2, tiled=True)  93.7 us
    all_gather x1, waiting for transfers between devices, body(): whole_right = lax.all_gather(right_block, 'seq', axis=0, tiled=True)  45.7 us
    dot_general x1, matrix products, body(): jnp.einsum('ij,jbc->ibc', left_block, trade_parts(spread, 'seq', 1, 0), p...  17.6 us
    convert_element_type x1, local copies, waits for them, and re-layouts, body(): values = shard_piece.astype(jnp.float32)  17.6 us
  transfers between devices with their start and end apart: 2, of which 2 were waited for; matrix products, arithmetic and copies ran while one was open for 0% of the time, Pallas kernels for 0%

profile of v1, /device:TPU:0, one launch (start us, length us, event | category | flops | bytes accessed | tf_op | source)
XLA Modules:
  0.0 659.7 jit_solution(13335346247552084549)
XLA Ops:
  6.5 0.0 copy-start
  6.5 0.0 all-gather.2.cloned.1.call-start
  6.5 0.7 all-gather.2.cloned.1.call-update
  7.3 0.7 convert_element_type.77
  8.0 45.7 %all-gather.2.cloned.1.call-done = bf16[1024,1024]{1,0:T(8,128)(2,1)} async-done(((bf16[64,1024]{1,0:T(8,128)(2,1)}), bf16[1024,1024]{1,0:T(8,128)(2,1)}) %all-gather.2.cloned.1.call-update) | async-done | bytes 2097168 | tf_op jit(solution)/shard_map/all_gather | solution.py:19
  53.7 12.9 %fusion.5 = bf16[8,1024,512]{2,1,0:T(8,128)(2,1)S(1)} fusion(bf16[8,1024,512]{2,1,0:T(8,128)(2,1)} %bitcast.104, f32[8,1024]{1,0:T(8,128)S(1)} %convert_element_type.77, bf16[1024,1024]{1,0:T(8,128)(2,1)} %all-gather.2.cloned.1.call-done), kind=kOutput, calls=%fused_computation.11 | convolution fusion | flops 8598323200 | bytes 18907136 | tf_op jit(solution)/shard_map/abc,bk->akc/dot_general | solution.py:20
  67.4 0.0 copy-start.1
  67.4 185.2 %all_to_all.23 = bf16[16,8,64,512]{3,2,1,0:T(8,128)(2,1)S(1)} all-to-all(bf16[16,8,64,512]{3,2,1,0:T(8,128)(2,1)S(1)} %fusion.16), channel_id=1, replica_groups=mesh['seq'=16,'ch'=2] {'seq'}, dimensions={0} | all-to-all | bytes 16777216 | tf_op jit(solution)/shard_map/all_to_all | solution.py:10
  252.7 0.0 copy-done.1
  252.7 17.6 %convert_bitcast_fusion.2 = bf16[128,64,512]{0,2,1:T(8,128)(2,1)} fusion(bf16[128,64,512]{2,1,0:T(8,128)(2,1)S(1)} %bitcast.103, bf16[128,128]{1,0:T(8,128)(2,1)S(1)} %copy-done.1), kind=kOutput, calls=%fused_computation.19 | convolution fusion | flops 1077936128 | bytes 16809984 | tf_op jit(solution)/shard_map/ij,jbc->ibc/dot_general | solution.py:24
  270.3 12.5 %copy.18 = bf16[128,64,512]{2,1,0:T(8,128)(2,1)} copy(bf16[128,64,512]{0,2,1:T(8,128)(2,1)} %convert_bitcast_fusion.2) | data formatting | bytes 16777216 | tf_op jit(solution)/shard_map/convert_element_type | solution.py:29
  282.8 187.8 %all_to_all.24 = bf16[128,64,512]{2,1,0:T(8,128)(2,1)} all-to-all(bf16[128,64,512]{2,1,0:T(8,128)(2,1)} %copy.18), channel_id=1, replica_groups=mesh['seq'=16,'ch'=2] {'seq'}, dimensions={0} | all-to-all | bytes 16777216 | tf_op jit(solution)/shard_map/all_to_all | solution.py:30
  470.6 0.0 slice-start
  470.6 11.7 %convert_bitcast_fusion.1 = f32[8,16,64,512]{3,2,0,1:T(8,128)} fusion(bf16[16,8,64,512]{3,2,1,0:T(8,128)(2,1)} %bitcast.101), kind=kLoop, calls=%fused_computation.9 | loop fusion | flops 4194304 | bytes 25165824 | tf_op jit(solution)/shard_map/convert_element_type | solution.py:31
  482.3 0.0 slice-start.1
  482.3 7.1 %copy.19 = f32[8,16,64,512]{3,2,1,0:T(8,128)S(1)} copy(f32[8,16,64,512]{3,2,0,1:T(8,128)} %convert_bitcast_fusion.1) | data formatting | bytes 33554432 | tf_op jit(solution)/shard_map/convert_element_type | solution.py:31
  489.4 0.0 slice-done
  489.4 0.0 slice-done.1
  489.5 7.0 %fusion.6 = bf16[2,4096,512]{2,1,0:T(8,128)(2,1)} fusion(f32[2,4096,512]{2,1,0:T(8,128)S(1)} %bitcast.100, bf16[2,4096,512]{2,1,0:T(8,128)(2,1)S(1)} %bitcast.107), kind=kLoop, calls=%fused_computation.13 | loop fusion | flops 29360128 | bytes 33554432 | tf_op jit(solution)/shard_map/convert_element_type | solution.py:31
  496.5 0.0 copy-start.2
  496.5 7.3 %all-to-all-start.2 = ((bf16[2,4096,512]{2,1,0:T(8,128)(2,1)}), bf16[2,4096,512]{2,1,0:T(8,128)(2,1)}, u32[]{:S(2)}, u32[]{:S(2)}) async-start(bf16[2,4096,512]{2,1,0:T(8,128)(2,1)} %fusion.6), calls=%async_computation.2 | async-start | bytes 16777216 | tf_op jit(solution)/shard_map/all_to_all | solution.py:36
  503.8 0.0 copy-done.2
  503.8 93.7 %all-to-all-done.2 = bf16[2,4096,512]{2,1,0:T(8,128)(2,1)} async-done(((bf16[2,4096,512]{2,1,0:T(8,128)(2,1)}), bf16[2,4096,512]{2,1,0:T(8,128)(2,1)}, u32[]{:S(2)}, u32[]{:S(2)}) %all-to-all-start.2) | async-done | bytes 8388640 | tf_op jit(solution)/shard_map/all_to_all | solution.py:36
  597.5 5.1 fusion
  602.6 11.5 %convert_bitcast_fusion = f32[1,4096,2,512]{3,1,2,0:T(8,128)} fusion(bf16[2,4096,512]{2,1,0:T(8,128)(2,1)} %all-to-all-done.2), kind=kLoop, calls=%fused_computation.3 | loop fusion | flops 4194304 | bytes 25165824 | tf_op jit(solution)/shard_map/convert_element_type | solution.py:37
  614.2 17.6 %copy.20 = f32[1,4096,2,512]{1,3,2,0:T(8,128)} copy(f32[1,4096,2,512]{3,1,2,0:T(8,128)} %convert_bitcast_fusion) | data formatting | bytes 33554432 | tf_op jit(solution)/shard_map/convert_element_type | solution.py:37
  631.7 0.0 copy-done
  631.7 9.2 %fusion.12 = bf16[4,4096,256]{1,2,0:T(8,128)(2,1)} fusion(bf16[4,256,256]{2,1,0:T(8,128)(2,1)S(1)} %copy-done, f32[4096,4,256]{0,2,1:T(8,128)} %bitcast.99, f32[4,256]{1,0:T(4,128)S(1)} %mul.58, f32[4096]{0:T(1024)S(1)} %add_rsqrt_fusion), kind=kOutput, calls=%fused_computation.20 | convolution fusion | flops 2164260864 | bytes 25710592 | tf_op jit(solution)/shard_map/otki,kij->otkj/dot_general | solution.py:43
  640.9 11.9 %copy.23 = bf16[4096,1024]{1,0:T(8,128)(2,1)} copy(bf16[4096,1024]{0,1:T(8,128)(2,1)} %bitcast.102) | data formatting | bytes 16777216 | tf_op jit(solution)/shard_map/reshape;reshape | solution.py:45
  (19 shorter events, 0.8 us)
Async XLA Ops:
  6.5 625.2 %copy-start = (bf16[4,256,256]{2,1,0:T(8,128)(2,1)S(1)}, bf16[4,256,256]{2,1,0:T(8,128)(2,1)}, u32[]{:S(2)}) copy-start(bf16[4,256,256]{2,1,0:T(8,128)(2,1)} %param.11) | copy-start | bytes 1572868
  6.5 47.2 %all-gather.2.cloned.1.call-start = ((), (), s32[]{:S(2)}) async-start(), calls=%async_computation.3 | async-start | bytes 2228224 | tf_op jit(solution)/shard_map/all_gather | solution.py:19
  67.4 185.2 %copy-start.1 = (bf16[128,128]{1,0:T(8,128)(2,1)S(1)}, bf16[128,128]{1,0:T(8,128)(2,1)}, u32[]{:S(2)}) copy-start(bf16[128,128]{1,0:T(8,128)(2,1)} %param.9) | copy-start | bytes 98308
  470.6 18.9 %slice-start = ((s8[8388608]{0:T(1024)(128)(4,1)}), s8[4194304]{0:T(1024)(128)(4,1)S(1)}, s32[]{:S(2)}) async-start(s8[8388608]{0:T(1024)(128)(4,1)} %bitcast.105), calls=%async_computation.4 | async-start | bytes 8388608
  482.3 7.1 %slice-start.1 = ((s8[8388608]{0:T(1024)(128)(4,1)}), s8[4194304]{0:T(1024)(128)(4,1)S(1)}, s32[]{:S(2)}) async-start(s8[8388608]{0:T(1024)(128)(4,1)} %bitcast.105), calls=%async_computation.5 | async-start | bytes 8388608
  496.5 7.3 %copy-start.2 = (f32[1024]{0:T(1024)S(1)}, f32[1024]{0:T(1024)}, u32[]{:S(2)}) copy-start(f32[1024]{0:T(1024)} %param.10) | copy-start | bytes 12292
  496.5 101.0 %all-to-all-start.2 = ((bf16[2,4096,512]{2,1,0:T(8,128)(2,1)}), bf16[2,4096,512]{2,1,0:T(8,128)(2,1)}, u32[]{:S(2)}, u32[]{:S(2)}) async-start(bf16[2,4096,512]{2,1,0:T(8,128)(2,1)} %fusion.6), calls=%async_computation.2 | async-start | bytes 16777216 | tf_op jit(solution)/shard_map/all_to_all | solution.py:36
Sparse Core Ops, SparseCore 0:
  9.5 44.1 all-gather.1
